TPU v7x, 32 devices: a whole 2x2x4 slice. The times are simulated.
32 devices in a mesh: line: 2 (over x), track: 16 (over z, y, core).
Axes of the slice: x: 2, y: 2, z: 4, core: 2. Of those that a mesh axis runs over, the one named last changes fastest.
Arguments:
- radiance: bfloat16 [2, 64, 224, 1000], P('line', 'track'), may hold values from -40 to 40, as said below
Outputs:
- cleaned: bfloat16 [2, 64, 224, 1000], P('line', 'track')
- filter_matrix: float32 [224, 224], replicated
Inputs may be any that keep to these rules, and one draw needn't show every extreme that they name: `radiance`: every flightline, band and column carries a column offset, a column gain and pixel noise, so no column is constant along track.
All inputs are finite; a program needn't handle non-finite values.
Results may differ from a plain program's by a relative error of at most 0.0045.
Values may be sent and summed in bfloat16 or wider, within the bound.
A program may use at most 64 MiB of HBM per device.

v0:
```python
import functools

import jax
import jax.numpy as jnp
from jax import lax
from jax.experimental import pallas as pl
from jax.experimental.pallas import tpu as pltpu
from jax.sharding import PartitionSpec as P

NCOMP = 40
ITERS = 4


EPSILON = 1e-05
HIGHEST = lax.Precision.HIGHEST


def from_behind(block, axis, distance):
    devices = range(lax.axis_size(axis))
    route = [(i - distance, i) for i in devices if i - distance in devices]
    return lax.ppermute(block, axis, route)


def column_terms(first_total, second_total, total_rows):
    col_mean = first_total / total_rows
    col_spread = jnp.sqrt(second_total / total_rows - col_mean * col_mean + EPSILON)
    band_mean = jnp.mean(col_mean, axis=1)
    factor = jnp.mean(col_spread, axis=1)[:, None] / col_spread
    return (col_mean, factor, band_mean)


PANEL = 32
GROUP = 8


def contract(left, right, left_axis, right_axis):
    return lax.dot_general(
        left, right, (((left_axis,), (right_axis,)), ((), ())),
        precision=HIGHEST, preferred_element_type=jnp.float32,
    )


def eliminate(panel, offset):
    size = panel.shape[0]
    row_ids = lax.broadcasted_iota(jnp.int32, (size, 128), 0)
    repeats = panel.shape[1] // 128
    tiles = [panel[:, t * 128:(t + 1) * 128] for t in range(repeats)]
    home, shift = divmod(offset, 128)
    scales = jnp.zeros((size, 128), jnp.float32)
    for start in range(0, size, GROUP):
        lanes = range(start, min(start + GROUP, size))
        columns = {}
        for k in lanes:
            tile, lane = divmod(offset + k, 128)
            columns[k] = jnp.broadcast_to(tiles[tile][:, lane:lane + 1], (size, 128))
        for k in lanes:
            pivot_row = jnp.broadcast_to(columns[k][k:k + 1], (size, 128))
            scales = jnp.where(row_ids == k, pivot_row, scales)
            step = jnp.where(row_ids > k, columns[k] * (1.0 / pivot_row), 0.0)
            for later in lanes:
                if later > k:
                    columns[later] = columns[later] - step * columns[later][k:k + 1]
            tiles = [tile - step * tile[k:k + 1] for tile in tiles]
    scales = 1.0 / jnp.sqrt(scales)
    return jnp.concatenate([tile * scales for tile in tiles], axis=1)


def mnf_kernel(signal_scale, noise_scale, kept, packed_ref, filter_ref, work):
    size = filter_ref.shape[0]
    wide = packed_ref.shape[0]
    packed = packed_ref[...]
    row_ids = lax.broadcasted_iota(jnp.int32, (wide, wide), 0)
    column_ids = lax.broadcasted_iota(jnp.int32, (wide, wide), 1)
    below = jnp.where((row_ids > column_ids) & (row_ids < size), packed, 0.0)
    above = jnp.where(row_ids < column_ids, packed, 0.0)
    diagonal = row_ids == column_ids
    noise = below + below.T + jnp.where(diagonal, packed, 0.0)
    signal = above + above.T + jnp.where(diagonal, packed[size:size + 1], 0.0)
    work[:, :wide] = noise[:size] * noise_scale
    work[:, wide:2 * wide] = jnp.where(diagonal, 1.0, 0.0)[:size]
    work[:, 2 * wide:] = signal[:size] * signal_scale
    for start in range(0, size, PANEL):
        end = min(start + PANEL, size)
        rows = eliminate(work[start:end, :], start)
        work[start:end, :] = rows
        if end < size:
            step = contract(rows[:, end:size], rows, 0, 0)
            work[end:, :] = work[end:, :] - step
    upper = work[:, :wide]
    upper = jnp.where(
        lax.broadcasted_iota(jnp.int32, (size, wide), 1)
        >= lax.broadcasted_iota(jnp.int32, (size, wide), 0),
        upper, 0.0,
    )
    inverse = work[:, wide:2 * wide]
    half_solved = work[:, 2 * wide:]
    margin = jnp.zeros((wide - size, wide), jnp.float32)
    inner = contract(
        jnp.concatenate([half_solved, margin], axis=0),
        jnp.concatenate([inverse, margin], axis=0), 1, 1,
    )
    whitened = 0.5 * (inner + inner.T)
    mapped = whitened[:kept]
    for iteration in range(ITERS):
        if iteration:
            mapped = contract(mapped, whitened, 1, 0)
        gram = contract(mapped, mapped, 1, 1)
        gram = jnp.concatenate([gram, jnp.zeros((kept, 128 - kept), jnp.float32)], axis=1)
        mapped = eliminate(jnp.concatenate([gram, mapped], axis=1), 0)[:, 128:]
    subspace = mapped[:, :size]
    forward = contract(subspace, inverse, 1, 0)
    backward = contract(subspace, upper, 1, 0)
    filter_ref[...] = contract(forward, backward, 0, 0)[:size, :size]


def mnf_filter(packed, size, signal_count, noise_count, kept):
    wide = packed.shape[0]
    return pl.pallas_call(
        functools.partial(mnf_kernel, 1.0 / signal_count, 1.0 / noise_count, kept),
        out_shape=jax.ShapeDtypeStruct((size, size), jnp.float32),
        in_specs=[pl.BlockSpec(memory_space=pltpu.VMEM)],
        out_specs=pl.BlockSpec(memory_space=pltpu.VMEM),
        scratch_shapes=[pltpu.VMEM((size, 3 * wide), jnp.float32)],
        name="mnf_filter",
    )(packed)


def track_place(track):
    return (lax.axis_index("line"), track)


def stats_kernel(tracks, x_ref, out_ref, paired, mine, slots, gathered, other, send, recv):
    chips = tracks // 2
    half = x_ref.shape[1] // 2
    width = x_ref.shape[2] // chips
    track = lax.axis_index("track")
    core, chip = lax.rem(track, 2), lax.div(track, 2)
    partner = track_place(chip * 2 + 1 - core)
    own_rows = pl.ds(pl.multiple_of(core * half, 8), half)
    other_rows = pl.ds(pl.multiple_of((1 - core) * half, 8), half)

    def ahead(step):
        q = lax.rem(chip + step, chips)
        return q, track_place(q * 2 + core), pl.ds(pl.multiple_of(q * width, 128), width)

    def copy(source, target, phase, sent, landed, device):
        return pltpu.make_async_remote_copy(
            src_ref=source, dst_ref=target, send_sem=send.at[phase, sent],
            recv_sem=recv.at[phase, landed], device_id=device,
            device_id_type=pl.DeviceIdType.MESH,
        )

    barrier = pltpu.get_barrier_semaphore()
    pl.semaphore_signal(barrier, inc=1, device_id=partner, device_id_type=pl.DeviceIdType.MESH)
    for step in range(1, chips):
        pl.semaphore_signal(
            barrier, inc=1, device_id=ahead(step)[1], device_id_type=pl.DeviceIdType.MESH
        )
    pl.semaphore_wait(barrier, chips)

    started = []
    for step in range(1, chips + 1):
        q, _, lanes = ahead(step)
        pair = copy(x_ref.at[:, other_rows, lanes], paired.at[q], 0, q, q, partner)
        pair.start()
        started.append(pair)
    for step in range(1, chips + 1):
        q, peer, lanes = ahead(step)
        started[step - 1].wait_recv()
        mine[q] = x_ref[:, own_rows, lanes] + paired[q]
        if step < chips:
            scatter = copy(mine.at[q], slots.at[chip], 1, q, chip, peer)
            scatter.start()
            started.append(scatter)
    total = mine[chip]
    for step in range(1, chips):
        q, peer, _ = ahead(chips - step)
        copy(mine.at[q], slots.at[q], 1, q, q, peer).wait_recv()
        total = total + slots[q]
    gathered[chip] = total
    for step in range(1, chips):
        q, peer, _ = ahead(step)
        gather = copy(gathered.at[chip], gathered.at[chip], 2, q, chip, peer)
        gather.start()
        started.append(gather)
    forward = copy(gathered.at[chip], other.at[chip], 3, chip, chip, partner)
    forward.start()
    started.append(forward)
    for step in range(1, chips):
        q, peer, _ = ahead(chips - step)
        copy(gathered.at[q], gathered.at[q], 2, q, q, peer).wait_recv()
        forward = copy(gathered.at[q], other.at[q], 3, q, q, partner)
        forward.start()
        started.append(forward)
    for q in range(chips):
        out_ref[:, own_rows, q * width:(q + 1) * width] = gathered[q]
    for q in range(chips):
        copy(other.at[q], other.at[q], 3, q, q, partner).wait_recv()
        out_ref[:, other_rows, q * width:(q + 1) * width] = other[q]
    for item in started:
        item.wait_send()


def stats_total(sums, tracks):
    chips = tracks // 2
    _, bands, lanes = sums.shape
    piece = (chips, 2, bands // 2, lanes // chips)
    return pl.pallas_call(
        functools.partial(stats_kernel, tracks),
        out_shape=jax.ShapeDtypeStruct(sums.shape, jnp.float32),
        in_specs=[pl.BlockSpec(memory_space=pltpu.VMEM)],
        out_specs=pl.BlockSpec(memory_space=pltpu.VMEM),
        scratch_shapes=[pltpu.VMEM(piece, jnp.float32)] * 5
        + [pltpu.SemaphoreType.DMA((4, chips))] * 2,
        compiler_params=pltpu.CompilerParams(collective_id=1, has_side_effects=True),
        name="stats_total",
    )(sums)


def gram_kernel(lines, tracks, x_ref, out_ref, slots, full, send, recv):
    count = lines * tracks
    me = lax.axis_index("line") * tracks + lax.axis_index("track")

    def ahead(step):
        peer = lax.rem(me + step, count)
        return peer, (lax.div(peer, tracks), lax.rem(peer, tracks))

    def settle(ref, sem):
        everyone = ref.at[pl.ds(0, count - 1)]
        pltpu.make_async_copy(everyone, everyone, sem).wait()

    barrier = pltpu.get_barrier_semaphore()

    @pl.loop(1, count)
    def _(step):
        pl.semaphore_signal(
            barrier, inc=1, device_id=ahead(step)[1], device_id_type=pl.DeviceIdType.MESH
        )

    pl.semaphore_wait(barrier, count - 1)

    @pl.loop(1, count)
    def _(step):
        peer, place = ahead(step)
        pltpu.make_async_remote_copy(
            src_ref=x_ref.at[peer], dst_ref=slots.at[me], send_sem=send.at[0],
            recv_sem=recv.at[0], device_id=place, device_id_type=pl.DeviceIdType.MESH,
        ).start()

    slots[me] = x_ref[me]
    settle(slots, recv.at[0])
    full[me] = jnp.sum(slots[...], axis=0)

    @pl.loop(1, count)
    def _(step):
        pltpu.make_async_remote_copy(
            src_ref=full.at[me], dst_ref=full.at[me], send_sem=send.at[1],
            recv_sem=recv.at[1], device_id=ahead(step)[1],
            device_id_type=pl.DeviceIdType.MESH,
        ).start()

    settle(full, recv.at[1])
    out_ref[...] = full[...]
    settle(x_ref, send.at[0])
    settle(full, send.at[1])


def gram_total(packed, lines, tracks):
    count = lines * tracks
    height, wide = packed.shape
    rows = -(-height // (8 * count)) * 8
    padded = jnp.pad(packed, ((0, count * rows - height), (0, 0)))
    piece = (count, rows, wide)
    total = pl.pallas_call(
        functools.partial(gram_kernel, lines, tracks),
        out_shape=jax.ShapeDtypeStruct(piece, jnp.float32),
        in_specs=[pl.BlockSpec(memory_space=pltpu.VMEM)],
        out_specs=pl.BlockSpec(memory_space=pltpu.VMEM),
        scratch_shapes=[pltpu.VMEM(piece, jnp.float32)] * 2
        + [pltpu.SemaphoreType.DMA((2,))] * 2,
        compiler_params=pltpu.CompilerParams(collective_id=0, has_side_effects=True),
        name="gram_total",
    )(padded.reshape(piece))
    return total.reshape(count * rows, wide)[:height]


def pack_grams(signal_part, noise_part, wide):
    size = signal_part.shape[0]
    above = jnp.arange(size)[:, None] < jnp.arange(size)[None, :]
    square = jnp.where(above, signal_part, noise_part)
    diagonal = jnp.sum(jnp.where(jnp.eye(size, dtype=bool), signal_part, 0.0), axis=0)
    packed = jnp.concatenate([square, diagonal[None]], axis=0)
    return jnp.pad(packed, ((0, wide - size - 1), (0, wide - size)))


def body(radiance):
    local_block = radiance[0]
    row_count = local_block.shape[0]
    column_count = local_block.shape[2]
    track_count = lax.axis_size("track")
    line_count = lax.axis_size("line")
    total_rows = row_count * track_count
    ahead = from_behind(local_block[:1], "track", -1)
    values = local_block.astype(jnp.float32)
    sums = jnp.stack([jnp.sum(values, axis=0), jnp.sum(values * values, axis=0)])
    strip = 128 * (track_count // 2)
    margin = -column_count % strip
    totals = stats_total(jnp.pad(sums, ((0, 0), (0, 0), (0, margin))), track_count)
    first_total, second_total = totals[0, :, :column_count], totals[1, :, :column_count]
    col_mean, factor, band_mean = column_terms(first_total, second_total, total_rows)
    centred = ((values - col_mean) * factor).astype(jnp.bfloat16)
    following = ((ahead.astype(jnp.float32) - col_mean) * factor).astype(jnp.bfloat16)
    rows_ahead = jnp.concatenate([centred[1:], following], axis=0)
    keep_last = lax.axis_index("track") < track_count - 1
    row_index = jnp.arange(row_count)
    row_keep = jnp.where((row_index < row_count - 1) | keep_last, 1.0, 0.0).astype(jnp.float32)
    differences = (
        (rows_ahead.astype(jnp.float32) - centred.astype(jnp.float32)) * row_keep[:, None, None]
    ).astype(jnp.bfloat16)
    signal_part = jnp.einsum("rbc,rdc->bd", centred, centred, preferred_element_type=jnp.float32)
    noise_part = jnp.einsum(
        "rbc,rdc->bd", differences, differences, preferred_element_type=jnp.float32
    )
    size = signal_part.shape[0]
    wide = (size // 128 + 1) * 128
    packed = gram_total(pack_grams(signal_part, noise_part, wide), line_count, track_count)
    signal_count = line_count * total_rows * column_count
    noise_count = 2 * line_count * (total_rows - 1) * column_count
    filter_matrix = mnf_filter(packed, size, signal_count, noise_count, NCOMP)
    narrow = filter_matrix.astype(jnp.bfloat16)
    mixed = jnp.einsum("ab,rac->rbc", narrow, centred, preferred_element_type=jnp.float32)
    cleaned = (band_mean[:, None] + mixed).astype(jnp.bfloat16)
    return (cleaned[None], filter_matrix)


def solution(mesh):
    in_specs = (P("line", "track", None, None),)
    out_specs = (P("line", "track", None, None), P())
    return jax.shard_map(body, mesh=mesh, in_specs=in_specs, out_specs=out_specs, check_vma=False)
```

profile of v0, /device:TPU:0, one launch (start us, length us, event | category | flops | bytes accessed | tf_op | source)
XLA Modules:
  0.0 114.2 jit_solution(1688661605312398245)
XLA Ops:
  0.6 0.0 copy-start
  0.6 1.2 %slice_bitcast_fusion = bf16[1,224,1000]{2,1,0:T(8,128)(2,1)S(1)} fusion(bf16[1,4,224,1000]{3,2,1,0:T(8,128)(2,1)} %param.1), kind=kLoop, calls=%fused_computation.28 | loop fusion | bytes 896000 | tf_op jit(solution)/shard_map/slice | solution.py:303
  1.8 1.3 %collective-permute-start = (bf16[1,224,1000]{2,1,0:T(8,128)(2,1)S(1)}, bf16[1,224,1000]{2,1,0:T(8,128)(2,1)S(1)}, u32[]{:S(2)}, u32[]{:S(2)}) collective-permute-start(bf16[1,224,1000]{2,1,0:T(8,128)(2,1)S(1)} %slice_bitcast_fusion), channel_id=1, source_target_pairs={{1,0},{2,1},{3,2},{4,3},{5,4},{6,5},{7,6},{8,7},{9,8},{10,9},{11,1... | collective-permute-start | bytes 1344008 | tf_op jit(solution)/shard_map/ppermute | solution.py:21
  3.1 2.0 %convert_reduce_fusion = f32[224,1000]{1,0:T(8,128)S(1)} fusion(bf16[1,4,224,1000]{3,2,1,0:T(8,128)(2,1)} %param.1), kind=kLoop, calls=%fused_computation.1 | loop fusion | flops 1568000 | bytes 2688000 | tf_op jit(solution)/shard_map/reduce_sum | solution.py:305
  5.1 0.4 fusion.2
  5.5 1.4 %select_maximum_fusion.x_ref = f32[2,224,1024]{2,1,0:T(8,128)} fusion(f32[1,224,1000]{2,1,0:T(8,128)S(1)} %bitcast.41, f32[1,224,1000]{2,1,0:T(8,128)S(1)} %bitcast.40), kind=kLoop, calls=%fused_computation.10 | loop fusion | flops 1835008 | bytes 3627008 | tf_op jit(solution)/shard_map/stack | solution.py:305
  6.9 47.0 %stats_total.1 = f32[2,224,1024]{2,1,0:T(8,128)} custom-call(f32[2,224,1024]{2,1,0:T(8,128)} %select_maximum_fusion.x_ref), custom_call_target="tpu_custom_call" | custom-call | tf_op jit(solution)/shard_map/stats_total/pallas_call | solution.py:208
  53.9 2.1 %fusion.15 = (f32[224]{0:T(256)S(1)}, f32[224]{0:T(256)S(1)}) fusion(f32[2,224,1024]{2,1,0:T(8,128)} %stats_total.1), kind=kLoop, calls=%fused_computation.27 | loop fusion | flops 1567552 | bytes 1793792 | tf_op jit(solution)/shard_map/reduce_sum | solution.py:27
  56.1 0.0 collective-permute-done
  56.1 1.8 %multiply_convert_fusion.6 = (bf16[1,224,1000]{2,1,0:T(8,128)(2,1)S(1)}, f32[224,1000]{1,0:T(8,128)S(1)}, f32[224,1000]{1,0:T(8,128)S(1)}) fusion(bf16[1,224,1000]{2,1,0:T(8,128)(2,1)S(1)} %collective-permute-done, f32[2,224,1024]{2,1,0:T(8,128)} %stats_total.1, f32[224]{0:T(256)S(1)} %broadcast_multiply_fusion), kind=kLoop, calls=%fused_computation.21 | loop fusion | flops 2240000 | bytes 4480896 | tf_op jit(solution)/shard_map/convert_element_type | solution.py:312
  57.9 0.6 fusion.4
  58.5 0.0 copy-start.1
  58.5 0.8 select_reduce_fusion
  59.3 0.5 copy-done.1
  59.7 0.1 slice.20
  59.8 0.1 copy.5
  60.0 3.4 %fusion.12 = f32[224,224]{0,1:T(8,128)S(1)} fusion(f32[224,224]{0,1:T(8,128)S(1)} %get-tuple-element.8, bf16[4,224,1000]{2,1,0:T(8,128)(2,1)} %copy-done.1, bf16[1,224,1000]{2,1,0:T(8,128)(2,1)S(1)} %get-tuple-element.4, bf16[3,224,1000]{2,1,0:T(8,128)(2,1)S(1)} %slice.20, f32[4]{0:T(128)S(1)} %or_select_fusion), kind=kOutput, calls=%fused_computation.19 | convolution fusion | flops 406884352 | bytes 3985424 | tf_op jit(solution)/shard_map/rbc,rdc->bd/dot_general | solution.py:321
  63.4 0.0 copy-start.2
  63.4 0.1 pad_maximum_fusion
  63.5 0.1 copy.10
  63.6 0.7 pad_bitcast_fusion.x_ref
  64.3 30.1 %gram_total.1 = f32[32,8,256]{2,1,0:T(8,128)} custom-call(f32[32,8,256]{2,1,0:T(8,128)} %pad_bitcast_fusion.x_ref), custom_call_target="tpu_custom_call" | custom-call | tf_op jit(solution)/shard_map/gram_total/pallas_call | solution.py:274
  94.5 16.7 %mnf_filter.1 = f32[224,224]{1,0:T(8,128)} custom-call(f32[256,256]{1,0:T(8,128)} %bitcast.42), custom_call_target="tpu_custom_call" | custom-call | tf_op jit(solution)/shard_map/mnf_filter/pallas_call | solution.py:118
  111.2 3.0 %fusion.10 = bf16[1,4,224,1000]{3,2,1,0:T(8,128)(2,1)} fusion(bf16[4,224,1000]{2,1,0:T(8,128)(2,1)S(1)} %copy-done.2, f32[224]{0:T(256)S(1)} %broadcast_multiply_fusion.1, f32[224,224]{1,0:T(8,128)} %mnf_filter.1), kind=kOutput, calls=%fused_computation.16 | convolution fusion | flops 403250176 | bytes 3785600 | tf_op jit(solution)/shard_map/ab,rac->rbc/dot_general | solution.py:331
  (5 shorter events, 0.0 us)
Async XLA Ops:
  0.6 4.5 %copy-start = (bf16[1,4,224,1000]{3,2,1,0:T(8,128)(2,1)S(1)}, bf16[1,4,224,1000]{3,2,1,0:T(8,128)(2,1)}, u32[]{:S(2)}) copy-start(bf16[1,4,224,1000]{3,2,1,0:T(8,128)(2,1)} %param.1) | copy-start | bytes 5376004
  1.8 54.2 %collective-permute-start = (bf16[1,224,1000]{2,1,0:T(8,128)(2,1)S(1)}, bf16[1,224,1000]{2,1,0:T(8,128)(2,1)S(1)}, u32[]{:S(2)}, u32[]{:S(2)}) collective-permute-start(bf16[1,224,1000]{2,1,0:T(8,128)(2,1)S(1)} %slice_bitcast_fusion), channel_id=1, source_target_pairs={{1,0},{2,1},{3,2},{4,3},{5,4},{6,5},{7,6},{8,7},{9,8},{10,9},{11,1... | collective-permute-start | bytes 1344008 | tf_op jit(solution)/shard_map/ppermute | solution.py:21
  58.5 1.2 %copy-start.1 = (bf16[4,224,1000]{2,1,0:T(8,128)(2,1)}, bf16[4,224,1000]{2,1,0:T(8,128)(2,1)S(1)}, u32[]{:S(2)}) copy-start(bf16[4,224,1000]{2,1,0:T(8,128)(2,1)S(1)} %fusion.4) | copy-start | bytes 5376004
  63.4 47.9 %copy-start.2 = (bf16[4,224,1000]{2,1,0:T(8,128)(2,1)S(1)}, bf16[4,224,1000]{2,1,0:T(8,128)(2,1)}, u32[]{:S(2)}) copy-start(bf16[4,224,1000]{2,1,0:T(8,128)(2,1)} %copy-done.1) | copy-start | bytes 5376004
where the time goes:
time: 115 us; the launch traced here: 114 us
  Pallas kernels  93.9 us (82%)
  other arithmetic  8.35 us (7%)
  matrix products  7.16 us (6%)
  local copies, waits for them, and re-layouts  2.72 us (2%)
  starting transfers between devices  1.29 us (1%)
    pallas_call x1, Pallas kernels, stats_total(): pl.pallas_call(functools.partial(stats_kernel, tracks), out_shape=jax.Sha...  47 us
    pallas_call x1, Pallas kernels, gram_total(): pl.pallas_call(functools.partial(gram_kernel, lines, tracks), out_shape=j...  30.1 us
    pallas_call x1, Pallas kernels, mnf_filter(): pl.pallas_call(functools.partial(mnf_kernel, 1.0 / signal_count, 1.0 / no...  16.7 us
    dot_general x1, matrix products, body(): jnp.einsum('rbc,rdc->bd', differences, differences, preferred_element_typ...  3.4 us
    dot_general x1, matrix products, body(): jnp.einsum('ab,rac->rbc', narrow, centred, preferred_element_type=jnp.flo...  3.01 us
  transfers between devices with their start and end apart: 1, of which 0 were waited for; matrix products, arithmetic and copies ran while one was open for 5% of the time, Pallas kernels for 41%

commit v1 on v0

v1 whole, which is shorter than its diff:
```python
import functools
import math

import jax
import jax.numpy as jnp
from jax import lax
from jax.experimental import pallas as pl
from jax.experimental.pallas import tpu as pltpu
from jax.sharding import PartitionSpec as P

NCOMP = 40
ITERS = 4


EPSILON = 1e-05
HIGHEST = lax.Precision.HIGHEST


PANEL = 32
GROUP = 8


def contract(left, right, left_axis, right_axis):
    return lax.dot_general(
        left, right, (((left_axis,), (right_axis,)), ((), ())),
        precision=HIGHEST, preferred_element_type=jnp.float32,
    )


def eliminate(panel, offset):
    size = panel.shape[0]
    row_ids = lax.broadcasted_iota(jnp.int32, (size, 128), 0)
    repeats = panel.shape[1] // 128
    tiles = [panel[:, t * 128:(t + 1) * 128] for t in range(repeats)]
    home, shift = divmod(offset, 128)
    scales = jnp.zeros((size, 128), jnp.float32)
    for start in range(0, size, GROUP):
        lanes = range(start, min(start + GROUP, size))
        columns = {}
        for k in lanes:
            tile, lane = divmod(offset + k, 128)
            columns[k] = jnp.broadcast_to(tiles[tile][:, lane:lane + 1], (size, 128))
        for k in lanes:
            pivot_row = jnp.broadcast_to(columns[k][k:k + 1], (size, 128))
            scales = jnp.where(row_ids == k, pivot_row, scales)
            step = jnp.where(row_ids > k, columns[k] * (1.0 / pivot_row), 0.0)
            for later in lanes:
                if later > k:
                    columns[later] = columns[later] - step * columns[later][k:k + 1]
            tiles = [tile - step * tile[k:k + 1] for tile in tiles]
    scales = 1.0 / jnp.sqrt(scales)
    return jnp.concatenate([tile * scales for tile in tiles], axis=1)


def mnf_kernel(signal_scale, noise_scale, kept, packed_ref, filter_ref, work):
    size = filter_ref.shape[0]
    wide = packed_ref.shape[0]
    packed = packed_ref[...]
    row_ids = lax.broadcasted_iota(jnp.int32, (wide, wide), 0)
    column_ids = lax.broadcasted_iota(jnp.int32, (wide, wide), 1)
    below = jnp.where((row_ids > column_ids) & (row_ids < size), packed, 0.0)
    above = jnp.where(row_ids < column_ids, packed, 0.0)
    diagonal = row_ids == column_ids
    noise = below + below.T + jnp.where(diagonal, packed, 0.0)
    signal = above + above.T + jnp.where(diagonal, packed[size:size + 1], 0.0)
    work[:, :wide] = noise[:size] * noise_scale
    work[:, wide:2 * wide] = jnp.where(diagonal, 1.0, 0.0)[:size]
    work[:, 2 * wide:] = signal[:size] * signal_scale
    for start in range(0, size, PANEL):
        end = min(start + PANEL, size)
        rows = eliminate(work[start:end, :], start)
        work[start:end, :] = rows
        if end < size:
            step = contract(rows[:, end:size], rows, 0, 0)
            work[end:, :] = work[end:, :] - step
    upper = work[:, :wide]
    upper = jnp.where(
        lax.broadcasted_iota(jnp.int32, (size, wide), 1)
        >= lax.broadcasted_iota(jnp.int32, (size, wide), 0),
        upper, 0.0,
    )
    inverse = work[:, wide:2 * wide]
    half_solved = work[:, 2 * wide:]
    margin = jnp.zeros((wide - size, wide), jnp.float32)
    inner = contract(
        jnp.concatenate([half_solved, margin], axis=0),
        jnp.concatenate([inverse, margin], axis=0), 1, 1,
    )
    whitened = 0.5 * (inner + inner.T)
    mapped = whitened[:kept]
    for iteration in range(ITERS):
        if iteration:
            mapped = contract(mapped, whitened, 1, 0)
        gram = contract(mapped, mapped, 1, 1)
        gram = jnp.concatenate([gram, jnp.zeros((kept, 128 - kept), jnp.float32)], axis=1)
        mapped = eliminate(jnp.concatenate([gram, mapped], axis=1), 0)[:, 128:]
    subspace = mapped[:, :size]
    forward = contract(subspace, inverse, 1, 0)
    backward = contract(subspace, upper, 1, 0)
    filter_ref[...] = contract(forward, backward, 0, 0)[:size, :size]


def mnf_filter(packed, size, signal_count, noise_count, kept):
    wide = packed.shape[0]
    return pl.pallas_call(
        functools.partial(mnf_kernel, 1.0 / signal_count, 1.0 / noise_count, kept),
        out_shape=jax.ShapeDtypeStruct((size, size), jnp.float32),
        in_specs=[pl.BlockSpec(memory_space=pltpu.VMEM)],
        out_specs=pl.BlockSpec(memory_space=pltpu.VMEM),
        scratch_shapes=[pltpu.VMEM((size, 3 * wide), jnp.float32)],
        name="mnf_filter",
    )(packed)


MESH = pl.DeviceIdType.MESH
VMEM_SPEC = pl.BlockSpec(memory_space=pltpu.VMEM)


def signal(semaphore, device):
    pl.semaphore_signal(semaphore, inc=1, device_id=device, device_id_type=MESH)


def merge(first, second, count):
    gap = second[0] - first[0]
    return first[0] + 0.5 * gap, first[1] + second[1] + (0.5 * count) * gap * gap


LIMIT = 40.0
FINE = 16.0
MEAN_STEP = 240.0 / math.log2(1.0 + LIMIT * FINE)
SPREAD_LOW, SPREAD_HIGH = math.log2(EPSILON), math.log2(LIMIT * LIMIT + 50.0)
SPREAD_STEP = 240.0 / (SPREAD_HIGH - SPREAD_LOW)
SPREAD_BASE = -0.5 * SPREAD_STEP * (SPREAD_HIGH + SPREAD_LOW)


def write_pair(ref, pair, count, *index):
    mean, total = pair
    code = jnp.exp2(MEAN_STEP * jnp.log2(1.0 + FINE * jnp.abs(mean)) - 120.0)
    ref[(*index, 0)] = jnp.where(mean < 0.0, -code, code).astype(ref.dtype)
    level = jnp.log2(total * (1.0 / count))
    ref[(*index, 1)] = jnp.exp2(SPREAD_STEP * level + SPREAD_BASE).astype(ref.dtype)


def read_codes(ref, *index):
    code = ref[(*index, 0)].astype(jnp.float32)
    size = jnp.exp2((jnp.log2(jnp.abs(code)) + 120.0) * (1.0 / MEAN_STEP)) - 1.0
    mean = jnp.where(code < 0.0, -size, size) * (1.0 / FINE)
    level = jnp.log2(ref[(*index, 1)].astype(jnp.float32)) - SPREAD_BASE
    return mean, level * (1.0 / SPREAD_STEP)


def read_pair(ref, count, *index):
    mean, level = read_codes(ref, *index)
    return mean, jnp.exp2(level) * count


def stats_kernel(
    tracks, x_ref, mean_ref, spread_ref, ahead_ref,
    out0, in0, own, out1, in1, out2, in2, gathered, other, send, recv, row_sem,
):
    chips = tracks // 2
    depth = chips // 2
    rows, bands, columns = x_ref.shape
    half = bands // 2
    width = in0.shape[-1]
    line = lax.axis_index("line")
    track = lax.axis_index("track")
    core, chip = lax.rem(track, 2), lax.div(track, 2)
    side, place = lax.rem(chip, 2), lax.div(chip, 2)
    own_rows = pl.ds(pl.multiple_of(core * half, 16), half)
    other_rows = pl.ds(pl.multiple_of((1 - core) * half, 16), half)
    partner = (line, chip * 2 + 1 - core)
    across = (line, (place * 2 + 1 - side) * 2 + core)

    def along(step):
        spot = lax.rem(place + step, depth)
        return spot, (line, (spot * 2 + side) * 2 + core)

    def copy(source, target, phase, sent, landed, device):
        return pltpu.make_async_remote_copy(
            src_ref=source, dst_ref=target, send_sem=send.at[phase, sent],
            recv_sem=recv.at[phase, landed], device_id=device, device_id_type=MESH,
        )

    def row_copy(device):
        return pltpu.make_async_remote_copy(
            src_ref=x_ref.at[0], dst_ref=ahead_ref, send_sem=row_sem.at[0],
            recv_sem=row_sem.at[1], device_id=device, device_id_type=MESH,
        )

    barrier = pltpu.get_barrier_semaphore()
    signal(barrier, partner)
    signal(barrier, across)
    for step in range(1, depth):
        signal(barrier, along(step)[1])
    has_before, has_after = track > 0, track < tracks - 1

    @pl.when(has_before)
    def _():
        signal(barrier, (line, track - 1))

    @pl.when(has_after)
    def _():
        signal(barrier, (line, track + 1))

    def local(band_rows, q):
        low = q * width
        high = min(low + width, columns)
        values = [x_ref[r, band_rows, low:high].astype(jnp.float32) for r in range(rows)]
        mean = sum(values[1:], values[0]) * (1.0 / rows)
        gaps = [value - mean for value in values]
        pair = mean, sum([gap * gap for gap in gaps], rows * EPSILON)
        if high - low < width:
            blank = jnp.ones((half, width - high + low), jnp.float32)
            pair = tuple(jnp.concatenate([item, blank], axis=1) for item in pair)
        return pair

    for q in range(chips):
        write_pair(out0, local(other_rows, q), rows, q)
    pl.semaphore_wait(barrier, depth + 1 + has_before.astype(jnp.int32) + has_after.astype(jnp.int32))

    started = []

    def launch(item):
        item.start()
        started.append(item)

    far = [(lax.rem(place + step, depth)) for step in range(1, depth + 1)]
    order = [spot * 2 + 1 - side for spot in far] + [spot * 2 + side for spot in far]
    for q in order:
        launch(copy(out0.at[q], in0.at[q], 0, q, q, partner))
    for q in range(chips):
        for k, item in enumerate(local(own_rows, q)):
            own[q, k] = item
    for spot in far:
        q = spot * 2 + 1 - side
        copy(in0.at[q], in0.at[q], 0, q, q, partner).wait_recv()
        pair = merge((own[q, 0], own[q, 1]), read_pair(in0, rows, q), rows)
        write_pair(out1, pair, 2 * rows, spot)
        launch(copy(out1.at[spot], in1.at[spot], 1, spot, spot, across))

    @pl.when(has_before)
    def _():
        row_copy((line, track - 1)).start()

    for step, spot in enumerate(far, 1):
        q = spot * 2 + side
        copy(in0.at[q], in0.at[q], 0, q, q, partner).wait_recv()
        pair = merge((own[q, 0], own[q, 1]), read_pair(in0, rows, q), rows)
        copy(in1.at[spot], in1.at[spot], 1, spot, spot, across).wait_recv()
        pair = merge(pair, read_pair(in1, 2 * rows, spot), 2 * rows)
        if step < depth:
            write_pair(out2, pair, 4 * rows, spot)
            launch(copy(out2.at[spot], in2.at[place], 2, spot, place, along(step)[1]))
    groups = [pair]
    for step in range(1, depth):
        spot, peer = along(step)
        copy(in2.at[spot], in2.at[spot], 2, spot, spot, peer).wait_recv()
        groups.append(read_pair(in2, 4 * rows, spot))
    mean = sum([group[0] for group in groups[1:]], groups[0][0]) * (1.0 / depth)
    total = sum([group[1] for group in groups[1:]], groups[0][1])
    for group in groups:
        total = total + (4.0 * rows) * (group[0] - mean) * (group[0] - mean)
    write_pair(gathered, (mean, total), tracks * rows, chip)

    def relay(q):
        launch(copy(gathered.at[q], other.at[q], 5, q, q, partner))

    def settle(ref, q, band_rows):
        mean, level = read_codes(ref, q)
        mean_ref[q, band_rows, :] = mean
        spread_ref[q, band_rows, :] = jnp.exp2(0.5 * level)

    for step in range(1, depth):
        launch(copy(gathered.at[chip], gathered.at[chip], 3, step, chip, along(step)[1]))
    for step in range(depth):
        spot, peer = along(step)
        q = spot * 2 + side
        if step:
            copy(gathered.at[q], gathered.at[q], 3, q, q, peer).wait_recv()
        launch(copy(gathered.at[q], gathered.at[q], 4, q, q, across))
        relay(q)
        settle(gathered, q, own_rows)
    for step in range(depth):
        q = along(step)[0] * 2 + 1 - side
        copy(gathered.at[q], gathered.at[q], 4, q, q, across).wait_recv()
        relay(q)
        settle(gathered, q, own_rows)
    for last in (side, 1 - side):
        for step in range(depth):
            q = along(step)[0] * 2 + last
            copy(other.at[q], other.at[q], 5, q, q, partner).wait_recv()
            settle(other, q, other_rows)

    @pl.when(has_after)
    def _():
        row_copy((line, track + 1)).wait_recv()

    @pl.when(jnp.logical_not(has_after))
    def _():
        ahead_ref[...] = x_ref[0]

    for item in started:
        item.wait_send()

    @pl.when(has_before)
    def _():
        row_copy((line, track - 1)).wait_send()


def column_stats(local_block, tracks):
    chips = tracks // 2
    depth = chips // 2
    _, bands, columns = local_block.shape
    width = -(-columns // (128 * chips)) * 128
    half = bands // 2

    def buffer(count, dtype=jnp.bfloat16):
        return pltpu.VMEM((count, 2, half, width), dtype)

    return pl.pallas_call(
        functools.partial(stats_kernel, tracks),
        out_shape=[
            jax.ShapeDtypeStruct((chips, bands, width), jnp.float32),
            jax.ShapeDtypeStruct((chips, bands, width), jnp.float32),
            jax.ShapeDtypeStruct((bands, columns), jnp.bfloat16),
        ],
        in_specs=[VMEM_SPEC],
        out_specs=[VMEM_SPEC] * 3,
        scratch_shapes=[buffer(chips), buffer(chips), buffer(chips, jnp.float32)]
        + [buffer(depth)] * 4 + [buffer(chips)] * 2
        + [pltpu.SemaphoreType.DMA((6, chips))] * 2 + [pltpu.SemaphoreType.DMA((2,))],
        compiler_params=pltpu.CompilerParams(collective_id=1, has_side_effects=True),
        name="column_stats",
    )(local_block)


def centre_kernel(
    keep_ref, x_ref, mean_ref, spread_ref, ahead_ref,
    centred_ref, band_ref, packed_ref, work, change,
):
    rows, bands, columns = x_ref.shape
    chips, _, width = mean_ref.shape
    band_mean = jnp.zeros((bands, 1), jnp.float32)
    band_spread = jnp.zeros((bands, 1), jnp.float32)
    for q in range(chips):
        span = min(width, columns - q * width)
        band_mean += jnp.sum(mean_ref[q, :, :span], axis=1, keepdims=True)
        band_spread += jnp.sum(spread_ref[q, :, :span], axis=1, keepdims=True)
    band_ref[...] = band_mean * (1.0 / columns)
    band_spread = band_spread * (1.0 / columns)
    for q in range(chips):
        low = q * width
        high = min(low + width, columns)
        span = high - low
        mean = mean_ref[q, :, :span]
        factor = band_spread / spread_ref[q, :, :span]

        def rounded(values):
            return ((values.astype(jnp.float32) - mean) * factor).astype(jnp.bfloat16)

        now = rounded(x_ref[0, :, low:high])
        for r in range(rows):
            work[r, :, low:high] = now
            centred_ref[r, :, low:high] = now
            later = rounded(x_ref[r + 1, :, low:high] if r + 1 < rows else ahead_ref[:, low:high])
            step = later.astype(jnp.float32) - now.astype(jnp.float32)
            if r + 1 == rows:
                step = step * keep_ref[0]
            change[r, :, low:high] = step.astype(jnp.bfloat16)
            now = later
    full = chips * width
    if full > columns:
        blank = jnp.zeros((rows, bands, full - columns), jnp.bfloat16)
        work[:, :, columns:] = blank
        change[:, :, columns:] = blank

    def gram(ref):
        total = jnp.zeros((bands, bands), jnp.float32)
        for r in range(rows):
            total += lax.dot_general(
                ref[r], ref[r], (((1,), (1,)), ((), ())), preferred_element_type=jnp.float32
            )
        return total

    signal_part, noise_part = gram(work), gram(change)
    row_ids = lax.broadcasted_iota(jnp.int32, (bands, bands), 0)
    column_ids = lax.broadcasted_iota(jnp.int32, (bands, bands), 1)
    diagonal = jnp.sum(
        jnp.where(row_ids == column_ids, signal_part, 0.0), axis=0, keepdims=True
    )
    packed_ref[...] = jnp.zeros(packed_ref.shape, jnp.float32)
    packed_ref[:bands, :bands] = jnp.where(row_ids < column_ids, signal_part, noise_part)
    packed_ref[bands:bands + 1, :bands] = diagonal


def centre(keep, local_block, mean, spread, ahead, height, wide):
    rows, bands, columns = local_block.shape
    full = mean.shape[0] * mean.shape[2]
    return pl.pallas_call(
        centre_kernel,
        out_shape=[
            jax.ShapeDtypeStruct(local_block.shape, jnp.bfloat16),
            jax.ShapeDtypeStruct((bands, 1), jnp.float32),
            jax.ShapeDtypeStruct((height, wide), jnp.float32),
        ],
        in_specs=[pl.BlockSpec(memory_space=pltpu.SMEM)] + [VMEM_SPEC] * 4,
        out_specs=[VMEM_SPEC] * 3,
        scratch_shapes=[pltpu.VMEM((rows, bands, full), jnp.bfloat16)] * 2,
        name="centre",
    )(keep, local_block, mean, spread, ahead)


def gram_kernel(lines, tracks, x_ref, out_ref, in0, mine, in1, total, in2, gathered, in3, send, recv):
    depth = tracks // 4
    line = lax.axis_index("line")
    track = lax.axis_index("track")
    core, chip = lax.rem(track, 2), lax.div(track, 2)
    side, place = lax.rem(chip, 2), lax.div(chip, 2)
    plane = lines * 2
    me = line * 2 + side
    partner = (line, chip * 2 + 1 - core)

    def beside(step):
        spot = lax.rem(me + step, plane)
        return spot, (lax.div(spot, 2), (place * 2 + lax.rem(spot, 2)) * 2 + core)

    def along(step):
        spot = lax.rem(place + step, depth)
        return spot, (line, (spot * 2 + side) * 2 + core)

    def copy(source, target, phase, sent, landed, device):
        return pltpu.make_async_remote_copy(
            src_ref=source, dst_ref=target, send_sem=send.at[phase, sent],
            recv_sem=recv.at[phase, landed], device_id=device, device_id_type=MESH,
        )

    barrier = pltpu.get_barrier_semaphore()
    signal(barrier, partner)
    for step in range(1, plane):
        signal(barrier, beside(step)[1])
    for step in range(1, depth):
        signal(barrier, along(step)[1])
    pl.semaphore_wait(barrier, plane + depth - 1)

    started = []

    def launch(item):
        item.start()
        started.append(item)

    for step in range(1, plane + 1):
        spot = beside(step)[0]
        launch(copy(x_ref.at[1 - core, spot], in0.at[spot], 0, spot, spot, partner))
    for step in range(1, plane + 1):
        spot, peer = beside(step)
        copy(in0.at[spot], in0.at[spot], 0, spot, spot, partner).wait_recv()
        mine[spot] = x_ref[core, spot] + in0[spot]
        if step < plane:
            launch(copy(mine.at[spot], in1.at[me], 1, spot, me, peer))
    piece = mine[me]
    for step in range(1, plane):
        spot, peer = beside(step)
        copy(in1.at[spot], in1.at[spot], 1, spot, spot, peer).wait_recv()
        piece = piece + in1[spot]
    total[...] = piece
    in2[place] = piece
    for step in range(1, depth):
        spot, peer = along(step)
        launch(copy(total, in2.at[place], 2, spot, place, peer))
    for step in range(1, depth):
        spot, peer = along(step)
        copy(in2.at[spot], in2.at[spot], 2, spot, spot, peer).wait_recv()
    piece = in2[0]
    for spot in range(1, depth):
        piece = piece + in2[spot]
    gathered[me] = piece
    for step in range(1, plane):
        launch(copy(gathered.at[me], gathered.at[me], 3, step, me, beside(step)[1]))
    launch(copy(gathered.at[me], in3.at[me], 4, me, me, partner))
    out_ref[core, me] = piece
    for step in range(1, plane):
        spot, peer = beside(step)
        copy(gathered.at[spot], gathered.at[spot], 3, spot, spot, peer).wait_recv()
        launch(copy(gathered.at[spot], in3.at[spot], 4, spot, spot, partner))
        out_ref[core, spot] = gathered[spot]
    for step in range(plane):
        spot = beside(step)[0]
        copy(in3.at[spot], in3.at[spot], 4, spot, spot, partner).wait_recv()
        out_ref[1 - core, spot] = in3[spot]
    for item in started:
        item.wait_send()


def gram_total(packed, lines, tracks):
    plane, depth = lines * 2, tracks // 4
    height, wide = packed.shape
    piece = (height // (2 * plane), wide)
    whole = (2, plane) + piece
    stack = pltpu.VMEM((plane,) + piece, jnp.float32)
    total = pl.pallas_call(
        functools.partial(gram_kernel, lines, tracks),
        out_shape=jax.ShapeDtypeStruct(whole, jnp.float32),
        in_specs=[VMEM_SPEC],
        out_specs=VMEM_SPEC,
        scratch_shapes=[
            stack, stack, stack, pltpu.VMEM(piece, jnp.float32),
            pltpu.VMEM((depth,) + piece, jnp.float32), stack, stack,
        ] + [pltpu.SemaphoreType.DMA((5, max(plane, depth)))] * 2,
        compiler_params=pltpu.CompilerParams(collective_id=0, has_side_effects=True),
        name="gram_total",
    )(packed.reshape(whole))
    return total.reshape(height, wide)


def body(radiance):
    local_block = radiance[0]
    row_count, size, column_count = local_block.shape
    track_count = lax.axis_size("track")
    line_count = lax.axis_size("line")
    total_rows = row_count * track_count
    mean, spread, ahead = column_stats(local_block, track_count)
    keep = (lax.axis_index("track") < track_count - 1).astype(jnp.float32).reshape(1)
    wide = (size // 128 + 1) * 128
    pieces = 16 * 2 * line_count
    height = -(-max(size + 1, wide) // pieces) * pieces
    centred, band_mean, packed = centre(keep, local_block, mean, spread, ahead, height, wide)
    packed = gram_total(packed, line_count, track_count)[:wide]
    signal_count = line_count * total_rows * column_count
    noise_count = 2 * line_count * (total_rows - 1) * column_count
    filter_matrix = mnf_filter(packed, size, signal_count, noise_count, NCOMP)
    narrow = filter_matrix.astype(jnp.bfloat16)
    mixed = jnp.einsum("ab,rac->rbc", narrow, centred, preferred_element_type=jnp.float32)
    cleaned = (band_mean + mixed).astype(jnp.bfloat16)
    return (cleaned[None], filter_matrix)


def solution(mesh):
    in_specs = (P("line", "track", None, None),)
    out_specs = (P("line", "track", None, None), P())
    return jax.shard_map(body, mesh=mesh, in_specs=in_specs, out_specs=out_specs, check_vma=False)
```

time: 115 us -> 80.6 us (0.70)
  Pallas kernels: 93.9 us -> 75.1 us
  other arithmetic: 8.35 us -> 1 us
  matrix products: 7.16 us -> 3.57 us
  local copies, waits for them, and re-layouts: 2.72 us -> 0 us
  starting transfers between devices: 1.29 us -> 0 us
    pallas_call x1, Pallas kernels: 30.1 us -> 18.9 us  [gram_total(): pl.pallas_call(functools.partial(gram_kernel, lines, tracks), out_shape=j...]
    pallas_call x1 -> x2, Pallas kernels: 47 us -> 39.5 us  [the longest x1 33.9 us: column_stats(): pl.pallas_call(functools.partial(stats_kernel, tracks), out_shape=[jax.Sh...]
    reduce_sum x3 -> x0, other arithmetic: 4.47 us -> none  [the longest x1 2.11 us: column_terms(): band_mean = jnp.mean(col_mean, axis=1)]
    dot_general x2 -> x0, matrix products: 4.15 us -> none  [the longest x1 3.4 us: body(): jnp.einsum('rbc,rdc->bd', differences, differences, preferred_element_typ...]
    convert_element_type x2 -> x0, other arithmetic: 2.4 us -> none  [the longest x1 1.82 us: body(): ((ahead.astype(jnp.float32) - col_mean) * factor).astype(jnp.bfloat16)]
    another operation x1 -> x0, other arithmetic: 1.37 us -> none  [body(): jnp.stack([jnp.sum(values, axis=0), jnp.sum(values * values, axis=0)])]
    ppermute x1 -> x0, starting transfers between devices: 1.29 us -> none  [from_behind(): return lax.ppermute(block, axis, route)]
    slice x2 -> x0, local copies, waits for them, and re-layouts: 1.28 us -> none  [the longest x1 1.18 us: body(): ahead = from_behind(local_block[:1], 'track', -1)]
  transfers between devices with their start and end apart: 1 -> 0, of which waited for: 0 -> 0; matrix products, arithmetic and copies ran while one was open for 5% -> 0% of each run, Pallas kernels for 41% -> 0%
where the time goes in v1:
time: 80.6 us; the launch traced here: 80.4 us
  Pallas kernels  75.1 us (93%)
  matrix products  3.57 us (4%)
  other arithmetic  1 us (1%)
    pallas_call x1, Pallas kernels, column_stats(): pl.pallas_call(functools.partial(stats_kernel, tracks), out_shape=[jax.Sh...  33.9 us
    pallas_call x1, Pallas kernels, gram_total(): pl.pallas_call(functools.partial(gram_kernel, lines, tracks), out_shape=j...  18.9 us
    pallas_call x1, Pallas kernels, mnf_filter(): pl.pallas_call(functools.partial(mnf_kernel, 1.0 / signal_count, 1.0 / no...  16.7 us
    pallas_call x1, Pallas kernels, centre(): pl.pallas_call(centre_kernel, out_shape=[jax.ShapeDtypeStruct(local_block...  5.65 us
    dot_general x1, matrix products, body(): jnp.einsum('ab,rac->rbc', narrow, centred, preferred_element_type=jnp.flo...  3.57 us

profile of v1, /device:TPU:0, one launch (start us, length us, event | category | flops | bytes accessed | tf_op | source)
XLA Modules:
  0.0 80.4 jit_solution(1137187396630341046)
XLA Ops:
  0.6 33.9 %column_stats.1 = (f32[8,224,128]{2,1,0:T(8,128)}, f32[8,224,128]{2,1,0:T(8,128)}, bf16[224,1000]{1,0:T(8,128)(2,1)}) custom-call(bf16[4,224,1000]{2,1,0:T(8,128)(2,1)} %bitcast.12), custom_call_target="tpu_custom_call" | custom-call | tf_op jit(solution)/shard_map/column_stats/pallas_call | solution.py:321
  34.5 5.6 %centre.1 = (bf16[4,224,1000]{2,1,0:T(8,128)(2,1)}, f32[224,1]{1,0:T(8,128)}, f32[256,256]{1,0:T(8,128)}) custom-call(f32[1]{0:T(128)} %bitcast.keep_ref, bf16[4,224,1000]{2,1,0:T(8,128)(2,1)} %bitcast.13, f32[8,224,128]{2,1,0:T(8,128)} %get-tuple-element.8.mean_ref, f32[8,224,128]{2,1,0:T(8,128)} %get-tuple-element.9.spread_ref, ...), custom_call_target="tpu_custom_call" | custom-call | tf_op jit(solution)/shard_map/centre/pallas_call | solution.py:400
  40.2 1.0 %reduce = f32[224]{0:T(256)S(1)} reduce(f32[224,1]{1,0:T(8,128)} %get-tuple-element.11, f32[]{:T(128)} %constant.7), dimensions={1}, to_apply=%get-tuple-element.11.reduce_sub_computation | reduce | bytes 1796 | tf_op jit(solution)/shard_map/centre/pallas_call | solution.py:400
  41.2 18.9 %gram_total.1 = f32[2,4,32,256]{3,2,1,0:T(8,128)} custom-call(f32[2,4,32,256]{3,2,1,0:T(8,128)} %bitcast.15), custom_call_target="tpu_custom_call" | custom-call | tf_op jit(solution)/shard_map/gram_total/pallas_call | solution.py:501
  60.1 16.7 %mnf_filter.1 = f32[224,224]{1,0:T(8,128)} custom-call(f32[256,256]{1,0:T(8,128)} %bitcast.14), custom_call_target="tpu_custom_call" | custom-call | tf_op jit(solution)/shard_map/mnf_filter/pallas_call | solution.py:105
  76.8 3.6 %fusion = bf16[1,4,224,1000]{3,2,1,0:T(8,128)(2,1)} fusion(bf16[4,224,1000]{2,1,0:T(8,128)(2,1)} %get-tuple-element.12, f32[224]{0:T(256)S(1)} %reduce, f32[224,224]{1,0:T(8,128)} %mnf_filter.1), kind=kOutput, calls=%fused_computation.1 | convolution fusion | flops 403250176 | bytes 3785600 | tf_op jit(solution)/shard_map/ab,rac->rbc/dot_general | solution.py:533

commit v2 on v1

--- a/solution.py
+++ b/solution.py
@@ -17,7 +17,7 @@
 
 
 PANEL = 32
-GROUP = 8
+GROUP = 16
 
 
 def contract(left, right, left_axis, right_axis):
@@ -27,32 +27,63 @@
     )
 
 
+def contract_fast(left, right, left_axis, right_axis):
+    dims = (((left_axis,), (right_axis,)), ((), ()))
+    high_left, high_right = left.astype(jnp.bfloat16), right.astype(jnp.bfloat16)
+    low_left = (left - high_left.astype(jnp.float32)).astype(jnp.bfloat16)
+    low_right = (right - high_right.astype(jnp.float32)).astype(jnp.bfloat16)
+
+    def dot(a, b):
+        return lax.dot_general(a, b, dims, preferred_element_type=jnp.float32)
+
+    return dot(high_left, high_right) + (dot(high_left, low_right) + dot(low_left, high_right))
+
+
 def eliminate(panel, offset):
     size = panel.shape[0]
-    row_ids = lax.broadcasted_iota(jnp.int32, (size, 128), 0)
-    repeats = panel.shape[1] // 128
-    tiles = [panel[:, t * 128:(t + 1) * 128] for t in range(repeats)]
-    home, shift = divmod(offset, 128)
-    scales = jnp.zeros((size, 128), jnp.float32)
+    row_ids = lax.broadcasted_iota(jnp.int32, (8, 128), 0)
+    repeats, pieces = panel.shape[1] // 128, size // 8
+    tiles = [
+        [panel[p * 8:(p + 1) * 8, t * 128:(t + 1) * 128] for p in range(pieces)]
+        for t in range(repeats)
+    ]
+    scales = [jnp.zeros((8, 128), jnp.float32)] * pieces
     for start in range(0, size, GROUP):
         lanes = range(start, min(start + GROUP, size))
         columns = {}
         for k in lanes:
             tile, lane = divmod(offset + k, 128)
-            columns[k] = jnp.broadcast_to(tiles[tile][:, lane:lane + 1], (size, 128))
+            columns[k] = [
+                jnp.broadcast_to(tiles[tile][p][:, lane:lane + 1], (8, 128))
+                if p >= k // 8 or k // 8 > p >= start // 8 else None for p in range(pieces)
+            ]
         for k in lanes:
-            pivot_row = jnp.broadcast_to(columns[k][k:k + 1], (size, 128))
-            scales = jnp.where(row_ids == k, pivot_row, scales)
-            step = jnp.where(row_ids > k, columns[k] * (1.0 / pivot_row), 0.0)
+            home, line = divmod(k, 8)
+            pivot_row = jnp.broadcast_to(columns[k][home][line:line + 1], (8, 128))
+            scales[home] = jnp.where(row_ids == line, pivot_row, scales[home])
+            inverse = 1.0 / pivot_row
+            steps = {p: columns[k][p] * inverse for p in range(home, pieces)}
+            steps[home] = jnp.where(row_ids > line, steps[home], 0.0)
+
+            def reduce(item):
+                row = jnp.broadcast_to(item[home][line:line + 1], (8, 128))
+                return [
+                    item[p] - steps[p] * row if p >= home else item[p] for p in range(pieces)
+                ]
+
             for later in lanes:
                 if later > k:
-                    columns[later] = columns[later] - step * columns[later][k:k + 1]
-            tiles = [tile - step * tile[k:k + 1] for tile in tiles]
-    scales = 1.0 / jnp.sqrt(scales)
-    return jnp.concatenate([tile * scales for tile in tiles], axis=1)
-
-
-def mnf_kernel(signal_scale, noise_scale, kept, packed_ref, filter_ref, work):
+                    columns[later] = reduce(columns[later])
+            tiles = [reduce(tile) for tile in tiles]
+    scales = [1.0 / jnp.sqrt(item) for item in scales]
+    return jnp.concatenate([
+        jnp.concatenate([tile[p] * scales[p] for tile in tiles], axis=1) for p in range(pieces)
+    ], axis=0)
+
+
+def mnf_kernel(
+    signal_scale, noise_scale, kept, packed_ref, filter_ref, narrow_ref, work, signal_work
+):
     size = filter_ref.shape[0]
     wide = packed_ref.shape[0]
     packed = packed_ref[...]
@@ -64,50 +95,57 @@
     noise = below + below.T + jnp.where(diagonal, packed, 0.0)
     signal = above + above.T + jnp.where(diagonal, packed[size:size + 1], 0.0)
     work[:, :wide] = noise[:size] * noise_scale
-    work[:, wide:2 * wide] = jnp.where(diagonal, 1.0, 0.0)[:size]
-    work[:, 2 * wide:] = signal[:size] * signal_scale
+    work[:, wide:] = jnp.where(diagonal, 1.0, 0.0)[:size]
+    signal_work[...] = signal * signal_scale
     for start in range(0, size, PANEL):
         end = min(start + PANEL, size)
-        rows = eliminate(work[start:end, :], start)
-        work[start:end, :] = rows
+        low = start // 128 * 128
+        high = wide + -(-end // 128) * 128
+        rows = eliminate(work[start:end, low:high], start - low)
+        work[start:end, low:high] = rows
         if end < size:
-            step = contract(rows[:, end:size], rows, 0, 0)
-            work[end:, :] = work[end:, :] - step
+            step = contract_fast(rows[:, end - low:size - low], rows, 0, 0)
+            work[end:, low:high] = work[end:, low:high] - step
     upper = work[:, :wide]
     upper = jnp.where(
         lax.broadcasted_iota(jnp.int32, (size, wide), 1)
         >= lax.broadcasted_iota(jnp.int32, (size, wide), 0),
         upper, 0.0,
     )
-    inverse = work[:, wide:2 * wide]
-    half_solved = work[:, 2 * wide:]
+    inverse = work[:, wide:]
     margin = jnp.zeros((wide - size, wide), jnp.float32)
-    inner = contract(
-        jnp.concatenate([half_solved, margin], axis=0),
-        jnp.concatenate([inverse, margin], axis=0), 1, 1,
-    )
+    inverse_full = jnp.concatenate([inverse, margin], axis=0)
+    half_solved = contract_fast(inverse_full, signal_work[...], 1, 0)
+    inner = contract_fast(half_solved, inverse_full, 1, 1)
     whitened = 0.5 * (inner + inner.T)
     mapped = whitened[:kept]
     for iteration in range(ITERS):
         if iteration:
-            mapped = contract(mapped, whitened, 1, 0)
-        gram = contract(mapped, mapped, 1, 1)
+            mapped = contract_fast(mapped, whitened, 1, 0)
+        gram = (contract if iteration + 1 == ITERS else contract_fast)(mapped, mapped, 1, 1)
         gram = jnp.concatenate([gram, jnp.zeros((kept, 128 - kept), jnp.float32)], axis=1)
         mapped = eliminate(jnp.concatenate([gram, mapped], axis=1), 0)[:, 128:]
     subspace = mapped[:, :size]
-    forward = contract(subspace, inverse, 1, 0)
-    backward = contract(subspace, upper, 1, 0)
-    filter_ref[...] = contract(forward, backward, 0, 0)[:size, :size]
+    forward = contract_fast(subspace, inverse, 1, 0)
+    backward = contract_fast(subspace, upper, 1, 0)
+    filter_matrix = contract_fast(forward, backward, 0, 0)
+    filter_ref[...] = filter_matrix[:size, :size]
+    narrow_ref[...] = filter_matrix.T[:size, :size].astype(jnp.bfloat16)
 
 
 def mnf_filter(packed, size, signal_count, noise_count, kept):
     wide = packed.shape[0]
     return pl.pallas_call(
         functools.partial(mnf_kernel, 1.0 / signal_count, 1.0 / noise_count, kept),
-        out_shape=jax.ShapeDtypeStruct((size, size), jnp.float32),
+        out_shape=[
+            jax.ShapeDtypeStruct((size, size), jnp.float32),
+            jax.ShapeDtypeStruct((size, size), jnp.bfloat16),
+        ],
         in_specs=[pl.BlockSpec(memory_space=pltpu.VMEM)],
-        out_specs=pl.BlockSpec(memory_space=pltpu.VMEM),
-        scratch_shapes=[pltpu.VMEM((size, 3 * wide), jnp.float32)],
+        out_specs=[pl.BlockSpec(memory_space=pltpu.VMEM)] * 2,
+        scratch_shapes=[
+            pltpu.VMEM((size, 2 * wide), jnp.float32), pltpu.VMEM((wide, wide), jnp.float32),
+        ],
         name="mnf_filter",
     )(packed)
 
@@ -156,7 +194,7 @@
 
 def stats_kernel(
     tracks, x_ref, mean_ref, spread_ref, ahead_ref,
-    out0, in0, own, out1, in1, out2, in2, gathered, other, send, recv, row_sem,
+    out0, in0, own, out1, in1, out2, in2, gathered, other, passing, send, recv, row_sem,
 ):
     chips = tracks // 2
     depth = chips // 2
@@ -182,26 +220,46 @@
             recv_sem=recv.at[phase, landed], device_id=device, device_id_type=MESH,
         )
 
-    def row_copy(device):
+    def row_copy(source, target, sent, landed, device):
         return pltpu.make_async_remote_copy(
-            src_ref=x_ref.at[0], dst_ref=ahead_ref, send_sem=row_sem.at[0],
-            recv_sem=row_sem.at[1], device_id=device, device_id_type=MESH,
+            src_ref=source, dst_ref=target, send_sem=row_sem.at[0, sent],
+            recv_sem=row_sem.at[1, landed], device_id=device, device_id_type=MESH,
         )
+
+    inner, outer = core == 1, core == 0
+    low_side, high_side = side == 0, side == 1
+    hands_down = outer & low_side & (place > 0)
+    passes_on = inner & low_side & (place < depth - 1)
+    has_after = track < tracks - 1
+    below = (line, (place * 2 - 2) * 2 + 1)
+    above = (line, (place * 2 + 2) * 2)
+    beyond = (line, place * 4 + 1)
+    to_partner = row_copy(x_ref.at[0], ahead_ref, 0, 0, partner)
+    to_below = row_copy(x_ref.at[0], passing, 1, 1, below)
+    to_across = row_copy(passing, ahead_ref, 1, 0, across)
+    to_beyond = row_copy(x_ref.at[0], ahead_ref, 0, 0, beyond)
 
     barrier = pltpu.get_barrier_semaphore()
     signal(barrier, partner)
     signal(barrier, across)
     for step in range(1, depth):
         signal(barrier, along(step)[1])
-    has_before, has_after = track > 0, track < tracks - 1
-
-    @pl.when(has_before)
-    def _():
-        signal(barrier, (line, track - 1))
-
-    @pl.when(has_after)
-    def _():
-        signal(barrier, (line, track + 1))
+
+    @pl.when(outer & high_side)
+    def _():
+        signal(barrier, beyond)
+
+    @pl.when(inner & low_side)
+    def _():
+        signal(barrier, (line, place * 4 + 2))
+
+    @pl.when(hands_down)
+    def _():
+        signal(barrier, below)
+
+    @pl.when(passes_on)
+    def _():
+        signal(barrier, above)
 
     def local(band_rows, q):
         low = q * width
@@ -217,7 +275,16 @@
 
     for q in range(chips):
         write_pair(out0, local(other_rows, q), rows, q)
-    pl.semaphore_wait(barrier, depth + 1 + has_before.astype(jnp.int32) + has_after.astype(jnp.int32))
+    greeted = (outer & high_side) | (inner & low_side)
+    relayed = hands_down | passes_on
+    pl.semaphore_wait(
+        barrier, depth + 1 + greeted.astype(jnp.int32) + relayed.astype(jnp.int32)
+    )
+
+    @pl.when(hands_down)
+    def _():
+        to_below.start()
+
 
     started = []
 
@@ -239,9 +306,18 @@
         write_pair(out1, pair, 2 * rows, spot)
         launch(copy(out1.at[spot], in1.at[spot], 1, spot, spot, across))
 
-    @pl.when(has_before)
-    def _():
-        row_copy((line, track - 1)).start()
+    @pl.when(inner)
+    def _():
+        to_partner.start()
+
+    @pl.when(outer & high_side)
+    def _():
+        to_beyond.start()
+
+    @pl.when(passes_on)
+    def _():
+        row_copy(x_ref.at[0], passing, 1, 1, above).wait_recv()
+        to_across.start()
 
     for step, spot in enumerate(far, 1):
         q = spot * 2 + side
@@ -294,7 +370,7 @@
 
     @pl.when(has_after)
     def _():
-        row_copy((line, track + 1)).wait_recv()
+        to_partner.wait_recv()
 
     @pl.when(jnp.logical_not(has_after))
     def _():
@@ -303,9 +379,21 @@
     for item in started:
         item.wait_send()
 
-    @pl.when(has_before)
-    def _():
-        row_copy((line, track - 1)).wait_send()
+    @pl.when(inner)
+    def _():
+        to_partner.wait_send()
+
+    @pl.when(outer & high_side)
+    def _():
+        to_beyond.wait_send()
+
+    @pl.when(hands_down)
+    def _():
+        to_below.wait_send()
+
+    @pl.when(passes_on)
+    def _():
+        to_across.wait_send()
 
 
 def column_stats(local_block, tracks):
@@ -329,7 +417,8 @@
         out_specs=[VMEM_SPEC] * 3,
         scratch_shapes=[buffer(chips), buffer(chips), buffer(chips, jnp.float32)]
         + [buffer(depth)] * 4 + [buffer(chips)] * 2
-        + [pltpu.SemaphoreType.DMA((6, chips))] * 2 + [pltpu.SemaphoreType.DMA((2,))],
+        + [pltpu.VMEM((bands, columns), jnp.bfloat16)]
+        + [pltpu.SemaphoreType.DMA((6, chips))] * 2 + [pltpu.SemaphoreType.DMA((2, 2))],
         compiler_params=pltpu.CompilerParams(collective_id=1, has_side_effects=True),
         name="column_stats",
     )(local_block)
@@ -513,6 +602,28 @@
     return total.reshape(height, wide)
 
 
+def restore_kernel(narrow_ref, band_ref, centred_ref, cleaned_ref):
+    mixed = jnp.dot(narrow_ref[...], centred_ref[0], preferred_element_type=jnp.float32)
+    cleaned_ref[0] = (band_ref[...] + mixed).astype(jnp.bfloat16)
+
+
+def restore(narrow, band_mean, centred):
+    rows, bands, columns = centred.shape
+    block = pl.BlockSpec((1, bands, columns), lambda r: (r, 0, 0))
+    return pl.pallas_call(
+        restore_kernel,
+        grid=(rows,),
+        out_shape=jax.ShapeDtypeStruct(centred.shape, jnp.bfloat16),
+        in_specs=[
+            pl.BlockSpec((bands, bands), lambda r: (0, 0)),
+            pl.BlockSpec((bands, 1), lambda r: (0, 0)),
+            block,
+        ],
+        out_specs=block,
+        name="restore",
+    )(narrow, band_mean, centred)
+
+
 def body(radiance):
     local_block = radiance[0]
     row_count, size, column_count = local_block.shape
@@ -528,10 +639,8 @@
     packed = gram_total(packed, line_count, track_count)[:wide]
     signal_count = line_count * total_rows * column_count
     noise_count = 2 * line_count * (total_rows - 1) * column_count
-    filter_matrix = mnf_filter(packed, size, signal_count, noise_count, NCOMP)
-    narrow = filter_matrix.astype(jnp.bfloat16)
-    mixed = jnp.einsum("ab,rac->rbc", narrow, centred, preferred_element_type=jnp.float32)
-    cleaned = (band_mean + mixed).astype(jnp.bfloat16)
+    filter_matrix, narrow = mnf_filter(packed, size, signal_count, noise_count, NCOMP)
+    cleaned = restore(narrow, band_mean, centred)
     return (cleaned[None], filter_matrix)
 
 

time: 80.6 us -> 75.5 us (0.937)
  matrix products: 3.57 us -> 0 us
  other arithmetic: 1 us -> 0 us
    pallas_call x1, Pallas kernels: 33.9 us -> 29.4 us  [column_stats(): pl.pallas_call(functools.partial(stats_kernel, tracks), out_shape=[jax.Sh...]
    pallas_call x0 -> x1, Pallas kernels: none -> 4.25 us  [restore(): pl.pallas_call(restore_kernel, grid=(rows,), out_shape=jax.ShapeDtypeStru...]
    dot_general x1 -> x0, matrix products: 3.57 us -> none  [body(): jnp.einsum('ab,rac->rbc', narrow, centred, preferred_element_type=jnp.flo...]
    pallas_call x1, Pallas kernels: 16.7 us -> 13.7 us  [mnf_filter(): pl.pallas_call(functools.partial(mnf_kernel, 1.0 / signal_count, 1.0 / no...]
    pallas_call x1, Pallas kernels: 18.9 us -> 21.6 us  [gram_total(): pl.pallas_call(functools.partial(gram_kernel, lines, tracks), out_shape=j...]
    pallas_call x1 -> x0, other arithmetic: 1 us -> none  [centre(): pl.pallas_call(centre_kernel, out_shape=[jax.ShapeDtypeStruct(local_block...]
where the time goes in v2:
time: 75.5 us; the launch traced here: 75.3 us
  Pallas kernels  74.6 us (99%)
    pallas_call x1, Pallas kernels, column_stats(): pl.pallas_call(functools.partial(stats_kernel, tracks), out_shape=[jax.Sh...  29.4 us
    pallas_call x1, Pallas kernels, gram_total(): pl.pallas_call(functools.partial(gram_kernel, lines, tracks), out_shape=j...  21.6 us
    pallas_call x1, Pallas kernels, mnf_filter(): pl.pallas_call(functools.partial(mnf_kernel, 1.0 / signal_count, 1.0 / no...  13.7 us
    pallas_call x1, Pallas kernels, centre(): pl.pallas_call(centre_kernel, out_shape=[jax.ShapeDtypeStruct(local_block...  5.65 us
    pallas_call x1, Pallas kernels, restore(): pl.pallas_call(restore_kernel, grid=(rows,), out_shape=jax.ShapeDtypeStru...  4.25 us

profile of v2, /device:TPU:0, one launch (start us, length us, event | category | flops | bytes accessed | tf_op | source)
XLA Modules:
  0.0 75.3 jit_solution(5970374968540941175)
XLA Ops:
  0.6 29.4 %column_stats.1 = (f32[8,224,128]{2,1,0:T(8,128)}, f32[8,224,128]{2,1,0:T(8,128)}, bf16[224,1000]{1,0:T(8,128)(2,1)}) custom-call(bf16[4,224,1000]{2,1,0:T(8,128)(2,1)} %bitcast.5), custom_call_target="tpu_custom_call" | custom-call | tf_op jit(solution)/shard_map/column_stats/pallas_call | solution.py:409
  30.1 5.6 %centre.1 = (bf16[4,224,1000]{2,1,0:T(8,128)(2,1)}, f32[224,1]{1,0:T(8,128)}, f32[256,256]{1,0:T(8,128)}) custom-call(f32[1]{0:T(128)} %bitcast.keep_ref, bf16[4,224,1000]{2,1,0:T(8,128)(2,1)} %bitcast.6, f32[8,224,128]{2,1,0:T(8,128)} %get-tuple-element.10.mean_ref, f32[8,224,128]{2,1,0:T(8,128)} %get-tuple-element.11.spread_ref, ...), custom_call_target="tpu_custom_call" | custom-call | tf_op jit(solution)/shard_map/centre/pallas_call | solution.py:489
  35.7 21.6 %gram_total.1 = f32[2,4,32,256]{3,2,1,0:T(8,128)} custom-call(f32[2,4,32,256]{3,2,1,0:T(8,128)} %bitcast.9), custom_call_target="tpu_custom_call" | custom-call | tf_op jit(solution)/shard_map/gram_total/pallas_call | solution.py:590
  57.3 13.7 %mnf_filter.1 = (f32[224,224]{1,0:T(8,128)}, bf16[224,224]{1,0:T(8,128)(2,1)}) custom-call(f32[256,256]{1,0:T(8,128)} %bitcast.8), custom_call_target="tpu_custom_call" | custom-call | tf_op jit(solution)/shard_map/mnf_filter/pallas_call | solution.py:138
  71.0 4.2 %restore.1 = bf16[4,224,1000]{2,1,0:T(8,128)(2,1)} custom-call(bf16[224,224]{1,0:T(8,128)(2,1)} %get-tuple-element.14.narrow_ref, f32[224,1]{1,0:T(8,128)} %get-tuple-element.15.band_ref, bf16[4,224,1000]{2,1,0:T(8,128)(2,1)} %get-tuple-element.16.centred_ref), custom_call_target="tpu_custom_call" | custom-call | tf_op jit(solution)/shard_map/restore/pallas_call | solution.py:613

commit v3 on v2

--- a/solution.py
+++ b/solution.py
@@ -192,8 +192,8 @@
     return mean, jnp.exp2(level) * count
 
 
-def stats_kernel(
-    tracks, x_ref, mean_ref, spread_ref, ahead_ref,
+def stats_part(
+    lines, tracks, x_ref, mean_ref, spread_ref, ahead_ref,
     out0, in0, own, out1, in1, out2, in2, gathered, other, passing, send, recv, row_sem,
 ):
     chips = tracks // 2
@@ -245,6 +245,11 @@
     for step in range(1, depth):
         signal(barrier, along(step)[1])
 
+    plane = lines * 2
+    for step in range(1, plane):
+        spot = lax.rem(line * 2 + side + step, plane)
+        signal(barrier, (lax.div(spot, 2), (place * 2 + lax.rem(spot, 2)) * 2 + core))
+
     @pl.when(outer & high_side)
     def _():
         signal(barrier, beyond)
@@ -278,7 +283,7 @@
     greeted = (outer & high_side) | (inner & low_side)
     relayed = hands_down | passes_on
     pl.semaphore_wait(
-        barrier, depth + 1 + greeted.astype(jnp.int32) + relayed.astype(jnp.int32)
+        barrier, depth + plane + greeted.astype(jnp.int32) + relayed.astype(jnp.int32)
     )
 
     @pl.when(hands_down)
@@ -376,57 +381,31 @@
     def _():
         ahead_ref[...] = x_ref[0]
 
-    for item in started:
-        item.wait_send()
-
-    @pl.when(inner)
-    def _():
-        to_partner.wait_send()
-
-    @pl.when(outer & high_side)
-    def _():
-        to_beyond.wait_send()
-
-    @pl.when(hands_down)
-    def _():
-        to_below.wait_send()
-
-    @pl.when(passes_on)
-    def _():
-        to_across.wait_send()
-
-
-def column_stats(local_block, tracks):
-    chips = tracks // 2
-    depth = chips // 2
-    _, bands, columns = local_block.shape
-    width = -(-columns // (128 * chips)) * 128
-    half = bands // 2
-
-    def buffer(count, dtype=jnp.bfloat16):
-        return pltpu.VMEM((count, 2, half, width), dtype)
-
-    return pl.pallas_call(
-        functools.partial(stats_kernel, tracks),
-        out_shape=[
-            jax.ShapeDtypeStruct((chips, bands, width), jnp.float32),
-            jax.ShapeDtypeStruct((chips, bands, width), jnp.float32),
-            jax.ShapeDtypeStruct((bands, columns), jnp.bfloat16),
-        ],
-        in_specs=[VMEM_SPEC],
-        out_specs=[VMEM_SPEC] * 3,
-        scratch_shapes=[buffer(chips), buffer(chips), buffer(chips, jnp.float32)]
-        + [buffer(depth)] * 4 + [buffer(chips)] * 2
-        + [pltpu.VMEM((bands, columns), jnp.bfloat16)]
-        + [pltpu.SemaphoreType.DMA((6, chips))] * 2 + [pltpu.SemaphoreType.DMA((2, 2))],
-        compiler_params=pltpu.CompilerParams(collective_id=1, has_side_effects=True),
-        name="column_stats",
-    )(local_block)
-
-
-def centre_kernel(
-    keep_ref, x_ref, mean_ref, spread_ref, ahead_ref,
-    centred_ref, band_ref, packed_ref, work, change,
+    def finish():
+        for item in started:
+            item.wait_send()
+
+        @pl.when(inner)
+        def _():
+            to_partner.wait_send()
+
+        @pl.when(outer & high_side)
+        def _():
+            to_beyond.wait_send()
+
+        @pl.when(hands_down)
+        def _():
+            to_below.wait_send()
+
+        @pl.when(passes_on)
+        def _():
+            to_across.wait_send()
+
+    return finish
+
+
+def centre_part(
+    keep, x_ref, mean_ref, spread_ref, ahead_ref, work, band_ref, packed_ref, change,
 ):
     rows, bands, columns = x_ref.shape
     chips, _, width = mean_ref.shape
@@ -451,11 +430,10 @@
         now = rounded(x_ref[0, :, low:high])
         for r in range(rows):
             work[r, :, low:high] = now
-            centred_ref[r, :, low:high] = now
             later = rounded(x_ref[r + 1, :, low:high] if r + 1 < rows else ahead_ref[:, low:high])
             step = later.astype(jnp.float32) - now.astype(jnp.float32)
             if r + 1 == rows:
-                step = step * keep_ref[0]
+                step = step * keep
             change[r, :, low:high] = step.astype(jnp.bfloat16)
             now = later
     full = chips * width
@@ -478,29 +456,20 @@
     diagonal = jnp.sum(
         jnp.where(row_ids == column_ids, signal_part, 0.0), axis=0, keepdims=True
     )
+    square = jnp.where(row_ids < column_ids, signal_part, noise_part)
+    halves, plane, depth, _ = packed_ref.shape
     packed_ref[...] = jnp.zeros(packed_ref.shape, jnp.float32)
-    packed_ref[:bands, :bands] = jnp.where(row_ids < column_ids, signal_part, noise_part)
-    packed_ref[bands:bands + 1, :bands] = diagonal
-
-
-def centre(keep, local_block, mean, spread, ahead, height, wide):
-    rows, bands, columns = local_block.shape
-    full = mean.shape[0] * mean.shape[2]
-    return pl.pallas_call(
-        centre_kernel,
-        out_shape=[
-            jax.ShapeDtypeStruct(local_block.shape, jnp.bfloat16),
-            jax.ShapeDtypeStruct((bands, 1), jnp.float32),
-            jax.ShapeDtypeStruct((height, wide), jnp.float32),
-        ],
-        in_specs=[pl.BlockSpec(memory_space=pltpu.SMEM)] + [VMEM_SPEC] * 4,
-        out_specs=[VMEM_SPEC] * 3,
-        scratch_shapes=[pltpu.VMEM((rows, bands, full), jnp.bfloat16)] * 2,
-        name="centre",
-    )(keep, local_block, mean, spread, ahead)
-
-
-def gram_kernel(lines, tracks, x_ref, out_ref, in0, mine, in1, total, in2, gathered, in3, send, recv):
+    for piece in range(halves * plane):
+        half, spot = divmod(piece, plane)
+        low = piece * depth
+        live = min(depth, bands - low)
+        if live > 0:
+            packed_ref[half, spot, :live, :bands] = square[low:low + live]
+        if low <= bands < low + depth:
+            packed_ref[half, spot, bands - low:bands - low + 1, :bands] = diagonal
+
+
+def gram_part(lines, tracks, x_ref, out_ref, in0, mine, in1, total, in2, gathered, in3, send, recv):
     depth = tracks // 4
     line = lax.axis_index("line")
     track = lax.axis_index("track")
@@ -523,14 +492,6 @@
             src_ref=source, dst_ref=target, send_sem=send.at[phase, sent],
             recv_sem=recv.at[phase, landed], device_id=device, device_id_type=MESH,
         )
-
-    barrier = pltpu.get_barrier_semaphore()
-    signal(barrier, partner)
-    for step in range(1, plane):
-        signal(barrier, beside(step)[1])
-    for step in range(1, depth):
-        signal(barrier, along(step)[1])
-    pl.semaphore_wait(barrier, plane + depth - 1)
 
     started = []
 
@@ -581,45 +542,72 @@
         item.wait_send()
 
 
-def gram_total(packed, lines, tracks):
-    plane, depth = lines * 2, tracks // 4
-    height, wide = packed.shape
+def campaign_kernel(lines, tracks, x_ref, centred_ref, band_ref, total_ref, *scratch):
+    mean, spread, ahead, change, packed = scratch[:5]
+    gram_scratch, stats_scratch = scratch[5:14], scratch[14:]
+    finish = stats_part(lines, tracks, x_ref, mean, spread, ahead, *stats_scratch)
+    keep = jnp.where(lax.axis_index("track") < tracks - 1, 1.0, 0.0)
+    centre_part(keep, x_ref, mean, spread, ahead, centred_ref, band_ref, packed, change)
+    gram_part(lines, tracks, packed, total_ref, *gram_scratch)
+    finish()
+
+
+def campaign(local_block, lines, tracks, height, wide):
+    chips, plane = tracks // 2, lines * 2
+    depth = chips // 2
+    rows, bands, columns = local_block.shape
+    width = -(-columns // (128 * chips)) * 128
+    full = chips * width
+    half = bands // 2
     piece = (height // (2 * plane), wide)
-    whole = (2, plane) + piece
+
+    def buffer(count, dtype=jnp.bfloat16):
+        return pltpu.VMEM((count, 2, half, width), dtype)
+
     stack = pltpu.VMEM((plane,) + piece, jnp.float32)
-    total = pl.pallas_call(
-        functools.partial(gram_kernel, lines, tracks),
-        out_shape=jax.ShapeDtypeStruct(whole, jnp.float32),
+    centred, band_mean, total = pl.pallas_call(
+        functools.partial(campaign_kernel, lines, tracks),
+        out_shape=[
+            jax.ShapeDtypeStruct((rows, bands, full), jnp.bfloat16),
+            jax.ShapeDtypeStruct((bands, 1), jnp.float32),
+            jax.ShapeDtypeStruct((2, plane) + piece, jnp.float32),
+        ],
         in_specs=[VMEM_SPEC],
-        out_specs=VMEM_SPEC,
-        scratch_shapes=[
-            stack, stack, stack, pltpu.VMEM(piece, jnp.float32),
-            pltpu.VMEM((depth,) + piece, jnp.float32), stack, stack,
-        ] + [pltpu.SemaphoreType.DMA((5, max(plane, depth)))] * 2,
+        out_specs=[VMEM_SPEC] * 3,
+        scratch_shapes=[pltpu.VMEM((chips, bands, width), jnp.float32)] * 2
+        + [pltpu.VMEM((bands, columns), jnp.bfloat16)]
+        + [pltpu.VMEM((rows, bands, full), jnp.bfloat16)]
+        + [pltpu.VMEM((2, plane) + piece, jnp.float32)]
+        + [stack, stack, stack, pltpu.VMEM(piece, jnp.float32)]
+        + [pltpu.VMEM((depth,) + piece, jnp.float32), stack, stack]
+        + [pltpu.SemaphoreType.DMA((5, max(plane, depth)))] * 2
+        + [buffer(chips), buffer(chips), buffer(chips, jnp.float32)]
+        + [buffer(depth)] * 4 + [buffer(chips)] * 2
+        + [pltpu.VMEM((bands, columns), jnp.bfloat16)]
+        + [pltpu.SemaphoreType.DMA((6, chips))] * 2 + [pltpu.SemaphoreType.DMA((2, 2))],
         compiler_params=pltpu.CompilerParams(collective_id=0, has_side_effects=True),
-        name="gram_total",
-    )(packed.reshape(whole))
-    return total.reshape(height, wide)
+        name="campaign",
+    )(local_block)
+    return centred, band_mean, total.reshape(height, wide)
 
 
 def restore_kernel(narrow_ref, band_ref, centred_ref, cleaned_ref):
     mixed = jnp.dot(narrow_ref[...], centred_ref[0], preferred_element_type=jnp.float32)
-    cleaned_ref[0] = (band_ref[...] + mixed).astype(jnp.bfloat16)
-
-
-def restore(narrow, band_mean, centred):
-    rows, bands, columns = centred.shape
-    block = pl.BlockSpec((1, bands, columns), lambda r: (r, 0, 0))
+    cleaned_ref[0] = (band_ref[...] + mixed[:, :cleaned_ref.shape[2]]).astype(jnp.bfloat16)
+
+
+def restore(narrow, band_mean, centred, columns):
+    rows, bands, full = centred.shape
     return pl.pallas_call(
         restore_kernel,
         grid=(rows,),
-        out_shape=jax.ShapeDtypeStruct(centred.shape, jnp.bfloat16),
+        out_shape=jax.ShapeDtypeStruct((rows, bands, columns), jnp.bfloat16),
         in_specs=[
             pl.BlockSpec((bands, bands), lambda r: (0, 0)),
             pl.BlockSpec((bands, 1), lambda r: (0, 0)),
-            block,
+            pl.BlockSpec((1, bands, full), lambda r: (r, 0, 0)),
         ],
-        out_specs=block,
+        out_specs=pl.BlockSpec((1, bands, columns), lambda r: (r, 0, 0)),
         name="restore",
     )(narrow, band_mean, centred)
 
@@ -630,17 +618,15 @@
     track_count = lax.axis_size("track")
     line_count = lax.axis_size("line")
     total_rows = row_count * track_count
-    mean, spread, ahead = column_stats(local_block, track_count)
-    keep = (lax.axis_index("track") < track_count - 1).astype(jnp.float32).reshape(1)
     wide = (size // 128 + 1) * 128
     pieces = 16 * 2 * line_count
     height = -(-max(size + 1, wide) // pieces) * pieces
-    centred, band_mean, packed = centre(keep, local_block, mean, spread, ahead, height, wide)
-    packed = gram_total(packed, line_count, track_count)[:wide]
+    centred, band_mean, packed = campaign(local_block, line_count, track_count, height, wide)
+    packed = packed[:wide]
     signal_count = line_count * total_rows * column_count
     noise_count = 2 * line_count * (total_rows - 1) * column_count
     filter_matrix, narrow = mnf_filter(packed, size, signal_count, noise_count, NCOMP)
-    cleaned = restore(narrow, band_mean, centred)
+    cleaned = restore(narrow, band_mean, centred, column_count)
     return (cleaned[None], filter_matrix)
 
 

time: 75.5 us -> 68.6 us (0.909)
  Pallas kernels: 74.6 us -> 67.7 us
    pallas_call x3 -> x1, Pallas kernels: 56.6 us -> 49.8 us  [campaign(): pl.pallas_call(functools.partial(campaign_kernel, lines, tracks), out_sha...]
where the time goes in v3:
time: 68.6 us; the launch traced here: 68.4 us
  Pallas kernels  67.7 us (99%)
    pallas_call x1, Pallas kernels, campaign(): pl.pallas_call(functools.partial(campaign_kernel, lines, tracks), out_sha...  49.8 us
    pallas_call x1, Pallas kernels, mnf_filter(): pl.pallas_call(functools.partial(mnf_kernel, 1.0 / signal_count, 1.0 / no...  13.7 us
    pallas_call x1, Pallas kernels, restore(): pl.pallas_call(restore_kernel, grid=(rows,), out_shape=jax.ShapeDtypeStru...  4.25 us

profile of v3, /device:TPU:0, one launch (start us, length us, event | category | flops | bytes accessed | tf_op | source)
XLA Modules:
  0.0 68.4 jit_solution(9093191077998721354)
XLA Ops:
  0.6 49.8 %campaign.1 = (bf16[4,224,1024]{2,1,0:T(8,128)(2,1)}, f32[224,1]{1,0:T(8,128)}, f32[2,4,32,256]{3,2,1,0:T(8,128)}) custom-call(bf16[4,224,1000]{2,1,0:T(8,128)(2,1)} %bitcast.3), custom_call_target="tpu_custom_call" | custom-call | tf_op jit(solution)/shard_map/campaign/pallas_call | solution.py:568
  50.4 13.7 %mnf_filter.1 = (f32[224,224]{1,0:T(8,128)}, bf16[224,224]{1,0:T(8,128)(2,1)}) custom-call(f32[256,256]{1,0:T(8,128)} %bitcast.5), custom_call_target="tpu_custom_call" | custom-call | tf_op jit(solution)/shard_map/mnf_filter/pallas_call | solution.py:138
  64.1 4.2 %restore.1 = bf16[4,224,1000]{2,1,0:T(8,128)(2,1)} custom-call(bf16[224,224]{1,0:T(8,128)(2,1)} %get-tuple-element.8.narrow_ref, f32[224,1]{1,0:T(8,128)} %get-tuple-element.9.band_ref, bf16[4,224,1024]{2,1,0:T(8,128)(2,1)} %get-tuple-element.10.centred_ref), custom_call_target="tpu_custom_call" | custom-call | tf_op jit(solution)/shard_map/restore/pallas_call | solution.py:601
